TPU v7x, 1024 devices: a whole 8x8x8 slice. The times are simulated.
1024 devices in a mesh: ctx: 64 (over z, x), ch: 16 (over y, core).
Axes of the slice: x: 8, y: 8, z: 8, core: 2. Of those that a mesh axis runs over, the one named last changes fastest.
Arguments:
- signal: bfloat16 [16384, 4096], P('ctx', 'ch'), may hold values from -6 to 6
- upstream: bfloat16 [16384, 8192], P('ctx', 'ch'), may hold values from -6 to 6
- out_weight: bfloat16 [4096, 8192], P(None, 'ch'), may hold values from -0.0625 to 0.0625
- residues: float32 [4096, 16], P('ch'), may hold values from -6 to 6
- decays: float32 [4096, 16], P('ch'), may hold values from 0.5 to 300
- skip_gain: float32 [4096], P('ch'), may hold values from 0.2 to 1
Outputs:
- grad_signal: bfloat16 [16384, 4096], P('ctx', 'ch')
- grad_residues: float32 [4096, 16], P('ch')
- grad_decays: float32 [4096, 16], P('ch')
- grad_skip: float32 [4096], P('ch')
All inputs are finite; a program needn't handle non-finite values.
Results may differ from a plain program's by a relative error of at most 0.019.
Values may be sent and summed in bfloat16 or wider, within the bound.
A program may use at most 32 MiB of HBM per device.

v0:
```python
import functools

import jax
import jax.numpy as jnp
from jax import lax
from jax.experimental import pallas as pl
from jax.experimental.pallas import tpu as pltpu
from jax.sharding import PartitionSpec as P

MESH = pl.DeviceIdType.MESH
F32 = jnp.float32
BF16 = jnp.bfloat16
RING = 8
PLUS_BLOCKS = (0, 1, 1, 3, 3, 5, 5)
MINUS_BLOCKS = (0, 2, 2, 4, 4, 6, 6)
SLOTS = len(PLUS_BLOCKS)


def kernel(
    sig_h, up_h, w_h, res_h, dec_h, skip_h,
    out, res_o, dec_o, skip_o,
    sig_v, up_v, w_v, res_v, dec_v, skip_v,
    sig_f, pair_s, pair_r, own, ring_s, ring_r, gc, yl,
    tile, rows_x, rows_z, local_in, back, full, state_in,
    local_sem, w_sem, pair_ss, pair_rs, ring_ss, ring_rs, x_ss, x_rs, z_ss, z_rs, b_ss, b_rs,
):
    tokens, width = sig_h.shape
    half_rows = tokens // 2
    lanes = width // 2
    modes = res_h.shape[0]
    length = tokens * RING * RING
    ctx = lax.axis_index("ctx")
    ch = lax.axis_index("ch")
    z, x = lax.div(ctx, RING), lax.rem(ctx, RING)
    y, core = lax.div(ch, 2), lax.rem(ch, 2)

    def at_x(step):
        return (z * RING + lax.rem(x + step, RING), ch)

    def at_z(step):
        return (lax.rem(z + step, RING) * RING + x, ch)

    def at_y(step):
        return (ctx, lax.rem(y + step, RING) * 2 + core)

    partner = (ctx, y * 2 + 1 - core)

    barrier = pltpu.get_barrier_semaphore()
    peers = [partner, at_y(1), at_y(RING - 1)]
    peers += [at_x(step) for step in range(1, RING)] + [at_z(step) for step in range(1, RING)]
    for peer in peers:
        pl.semaphore_signal(barrier, inc=1, device_id=peer, device_id_type=MESH)

    def w_copy(index):
        offset = lax.div(index + 1, 2)
        dest = lax.rem(y + 4 + (2 * lax.rem(index, 2) - 1) * -offset + RING, RING)
        return pltpu.make_async_copy(
            w_h.at[pl.ds(dest * 2 * width, 2 * width), :], w_v.at[index], w_sem.at[index]
        )

    loads = [
        pltpu.make_async_copy(src, dst, local_sem.at[n])
        for n, (src, dst) in enumerate(
            ((up_h, up_v), (dec_h, dec_v), (res_h, res_v), (skip_h, skip_v), (sig_h, sig_v))
        )
    ]
    loads[0].start()
    w_copy(jnp.int32(0)).start()
    w_copy(jnp.int32(1)).start()
    for load in loads[1:]:
        load.start()
    for index in range(2, RING):
        w_copy(jnp.int32(index)).start()

    loads[0].wait()

    def product(index, carry):
        w_copy(index).wait()
        theirs = w_v[index, pl.ds(pl.multiple_of((1 - core) * width, width), width), :]
        pair_s[index] = lax.dot_general(
            up_v[...], theirs, (((1,), (1,)), ((), ())), preferred_element_type=F32
        ).astype(BF16)
        mine = w_v[index, pl.ds(pl.multiple_of(core * width, width), width), :]
        own[index] = lax.dot_general(
            up_v[...], mine, (((1,), (1,)), ((), ())), preferred_element_type=F32
        )
        return carry

    lax.fori_loop(0, RING, product, 0)
    pl.semaphore_wait(barrier, len(peers))

    def pair_copy(index):
        return pltpu.make_async_remote_copy(
            src_ref=pair_s.at[index], dst_ref=pair_r.at[index],
            send_sem=pair_ss.at[index], recv_sem=pair_rs.at[index],
            device_id=partner, device_id_type=MESH,
        )

    def ring_copy(way, slot):
        return pltpu.make_async_remote_copy(
            src_ref=ring_s.at[way, slot], dst_ref=ring_r.at[way, slot],
            send_sem=ring_ss.at[way, slot], recv_sem=ring_rs.at[way, slot],
            device_id=at_y(1 if way == 0 else RING - 1), device_id_type=MESH,
        )

    for index in range(RING):
        pair_copy(index).start()
    arrived = set()

    def chip_sum(index, half):
        if index not in arrived:
            arrived.add(index)
            pair_copy(index).wait_recv()
        span = pl.ds(half * half_rows, half_rows)
        return own[index, span, :] + pair_r[index, span, :].astype(F32)

    def ring_step(slot):
        for way, blocks in enumerate((PLUS_BLOCKS, MINUS_BLOCKS)):
            total = chip_sum(blocks[slot], (slot + way) % 2)
            if slot >= 2:
                ring_copy(way, slot - 2).wait_recv()
                total = total + ring_r[way, slot - 2].astype(F32)
            ring_s[way, slot] = total.astype(BF16)
            ring_copy(way, slot).start()

    ring_step(0)
    ring_step(1)

    for load in loads[1:]:
        load.wait()
    pole = jnp.exp(dec_v[...] * (-1.0 / length))
    pole_block = jnp.exp(dec_v[...] * (-float(tokens) / length))
    gain = res_v[...] * (1.0 / length**0.5)
    sig_f[...] = sig_v[...].astype(F32)
    zero = jnp.zeros((modes, width), F32)

    def signal_steps(group, carry):
        state, slope = carry
        for step in range(8):
            row = sig_f[pl.ds(group * 8 + step, 1), :]
            state = (state + row) * pole
            slope = slope * pole + state
        return state, slope

    sig_state, sig_slope = lax.fori_loop(0, tokens // 8, signal_steps, (zero, zero))

    for slot in range(2, SLOTS):
        ring_step(slot)
    for half in (1, 0):
        total = chip_sum(RING - 1, half)
        for way in (0, 1):
            slot = SLOTS - 1 - (half + way) % 2
            ring_copy(way, slot).wait_recv()
            total = total + ring_r[way, slot].astype(F32)
        gc[pl.ds(half * half_rows, half_rows), :] = total.astype(BF16).astype(F32)

    skip_sum = jnp.sum(gc[...] * sig_f[...], axis=0, keepdims=True)

    def gradient_steps(group, carry):
        state, slope, res_sum, dec_sum = carry
        for step in range(8):
            pos = tokens - 1 - (group * 8 + step)
            grad = gc[pl.ds(pos, 1), :]
            row = sig_f[pl.ds(pos, 1), :]
            moved = state * pole
            state = grad + moved
            slope = slope * pole + moved
            res_sum = res_sum + row * state
            dec_sum = dec_sum + row * slope
            yl[pl.ds(pos, 1), :] = jnp.sum(gain * state, axis=0, keepdims=True)
        return state, slope, res_sum, dec_sum

    state, slope, res_sum, dec_sum = lax.fori_loop(
        0, tokens // 8, gradient_steps, (zero, zero, zero, zero)
    )

    parts = (
        state, slope, sig_state, sig_slope, res_sum, dec_sum,
        jnp.broadcast_to(skip_sum, (modes, width)), pole_block,
    )
    for line, part in enumerate(parts):
        for half in (0, 1):
            for first in range(0, modes, 8):
                tile[pl.ds((half * modes + first) * 8 + line, 8, stride=8), :] = part[
                    first : first + 8, half * lanes : (half + 1) * lanes
                ]
    share = 2 * modes // RING
    span = share * 8

    def x_copy(step):
        peer = lax.rem(x + step, RING)
        return pltpu.make_async_remote_copy(
            src_ref=tile.at[pl.ds(pl.multiple_of(peer * span, 8), span), :], dst_ref=rows_x.at[x],
            send_sem=x_ss.at[step], recv_sem=x_rs.at[step],
            device_id=at_x(step), device_id_type=MESH,
        )

    for step in range(1, RING):
        x_copy(step).start()
    rows_x[x] = tile[pl.ds(pl.multiple_of(x * span, 8), span), :]
    for step in range(1, RING):
        x_copy(step).wait_recv()

    def line_of(ref, index, line):
        return ref[index, pl.ds(line, share, stride=8), :]

    empty = jnp.zeros((share, lanes), F32)
    jump = line_of(rows_x, 0, 7)
    state, slope, res_sum, dec_sum, skip_sum = empty, empty, empty, empty, empty
    for block in reversed(range(RING)):
        local_in[block] = state
        sig_state, sig_slope = line_of(rows_x, block, 2), line_of(rows_x, block, 3)
        res_sum = res_sum + line_of(rows_x, block, 4) + state * sig_state
        dec_sum = dec_sum + line_of(rows_x, block, 5) + slope * sig_state + state * sig_slope
        skip_sum = skip_sum + line_of(rows_x, block, 6)
        slope = line_of(rows_x, block, 1) + jump * (slope + tokens * state)
        state = line_of(rows_x, block, 0) + jump * state
    sig_state, sig_slope = empty, empty
    for block in range(RING):
        sig_slope = line_of(rows_x, block, 3) + jump * (sig_slope + tokens * sig_state)
        sig_state = line_of(rows_x, block, 2) + jump * sig_state
    for line, part in enumerate((state, slope, sig_state, sig_slope, res_sum, dec_sum, skip_sum, jump)):
        rows_z[z, pl.ds(line, share, stride=8), :] = part

    def z_copy(step):
        return pltpu.make_async_remote_copy(
            src_ref=rows_z.at[z], dst_ref=rows_z.at[z],
            send_sem=z_ss.at[step], recv_sem=z_rs.at[step],
            device_id=at_z(step), device_id_type=MESH,
        )

    for step in range(1, RING):
        z_copy(step).start()
    for step in range(1, RING):
        z_copy(step).wait_recv()

    row_jump = jump * jump
    row_jump = row_jump * row_jump
    row_jump = row_jump * row_jump
    state, slope, res_sum, dec_sum, skip_sum, incoming = (empty,) * 6
    for row in reversed(range(RING)):
        incoming = jnp.where(z == row, state, incoming)
        sig_state, sig_slope = line_of(rows_z, row, 2), line_of(rows_z, row, 3)
        res_sum = res_sum + line_of(rows_z, row, 4) + state * sig_state
        dec_sum = dec_sum + line_of(rows_z, row, 5) + slope * sig_state + state * sig_slope
        skip_sum = skip_sum + line_of(rows_z, row, 6)
        slope = line_of(rows_z, row, 1) + row_jump * (slope + (tokens * RING) * state)
        state = line_of(rows_z, row, 0) + row_jump * state
    for block in reversed(range(RING)):
        back[block, 0:share, :] = local_in[block] + incoming
        back[block, share : 2 * share, :] = res_sum
        back[block, 2 * share : 3 * share, :] = dec_sum
        back[block, 3 * share : 4 * share, :] = skip_sum
        incoming = incoming * jump

    def b_copy(step):
        return pltpu.make_async_remote_copy(
            src_ref=back.at[lax.rem(x + step, RING)], dst_ref=full.at[x],
            send_sem=b_ss.at[step], recv_sem=b_rs.at[step],
            device_id=at_x(step), device_id_type=MESH,
        )

    for step in range(1, RING):
        b_copy(step).start()
    full[x] = back[x]
    for step in range(1, RING):
        b_copy(step).wait_recv()

    per_half = RING // 2
    for peer in range(RING):
        first, cols = (peer % per_half) * share, pl.ds((peer // per_half) * lanes, lanes)
        modes_here = pl.ds(first, share)
        state_in[modes_here, cols] = full[peer, 0:share, :]
        res_o[modes_here, cols] = full[peer, share : 2 * share, :] * (1.0 / length)
        dec_o[modes_here, cols] = full[peer, 2 * share : 3 * share, :] * (-1.0 / length) * (1.0 / length)
        if peer % per_half == 0:
            skip_o[:, cols] = full[peer, 3 * share : 3 * share + 1, :] * (1.0 / length**0.5)
    dec_o[...] = dec_o[...] * res_v[...]

    def late_steps(group, term):
        for step in range(8):
            pos = tokens - 1 - (group * 8 + step)
            term = term * pole
            here = pl.ds(pos, 1)
            yl[here, :] = yl[here, :] + jnp.sum(term, axis=0, keepdims=True)
        return term

    lax.fori_loop(0, tokens // 8, late_steps, gain * state_in[...])
    out[...] = (yl[...] + skip_v[...] * gc[...]).astype(BF16)

    for index in range(RING):
        pair_copy(index).wait_send()
    for slot in range(SLOTS):
        for way in (0, 1):
            ring_copy(way, slot).wait_send()
    for step in range(1, RING):
        x_copy(step).wait_send()
        z_copy(step).wait_send()
        b_copy(step).wait_send()


def body(signal, upstream, out_weight, residues, decays, skip_gain):
    tokens, width = signal.shape
    features = upstream.shape[1]
    modes = residues.shape[1]
    lanes = width // 2
    share = 2 * modes // RING
    any_ref = pl.BlockSpec(memory_space=pl.ANY)
    in_vmem = pl.BlockSpec(memory_space=pltpu.VMEM)
    dma = pltpu.SemaphoreType.DMA
    grad_signal, res_t, dec_t, skip = pl.pallas_call(
        kernel,
        out_shape=(
            jax.ShapeDtypeStruct((tokens, width), BF16),
            jax.ShapeDtypeStruct((modes, width), F32),
            jax.ShapeDtypeStruct((modes, width), F32),
            jax.ShapeDtypeStruct((1, width), F32),
        ),
        in_specs=[any_ref] * 6,
        out_specs=(in_vmem,) * 4,
        scratch_shapes=[
            pltpu.VMEM((tokens, width), BF16),
            pltpu.VMEM((tokens, features), BF16),
            pltpu.VMEM((RING, 2 * width, features), BF16),
            pltpu.VMEM((modes, width), F32),
            pltpu.VMEM((modes, width), F32),
            pltpu.VMEM((1, width), F32),
            pltpu.VMEM((tokens, width), F32),
            pltpu.VMEM((RING, tokens, width), BF16),
            pltpu.VMEM((RING, tokens, width), BF16),
            pltpu.VMEM((RING, tokens, width), F32),
            pltpu.VMEM((2, SLOTS, tokens // 2, width), BF16),
            pltpu.VMEM((2, SLOTS, tokens // 2, width), BF16),
            pltpu.VMEM((tokens, width), F32),
            pltpu.VMEM((tokens, width), F32),
            pltpu.VMEM((2 * modes * 8, lanes), F32),
            pltpu.VMEM((RING, share * 8, lanes), F32),
            pltpu.VMEM((RING, share * 8, lanes), F32),
            pltpu.VMEM((RING, share, lanes), F32),
            pltpu.VMEM((RING, share * 4, lanes), F32),
            pltpu.VMEM((RING, share * 4, lanes), F32),
            pltpu.VMEM((modes, width), F32),
            dma((5,)), dma((RING,)), dma((RING,)), dma((RING,)),
            dma((2, SLOTS)), dma((2, SLOTS)),
            dma((RING,)), dma((RING,)), dma((RING,)), dma((RING,)), dma((RING,)), dma((RING,)),
        ],
        compiler_params=pltpu.CompilerParams(collective_id=0, has_side_effects=True),
    )(signal, upstream, out_weight, residues.T, decays.T, skip_gain.reshape(1, width))
    return grad_signal, res_t.T, dec_t.T, skip.reshape(width)


def solution(mesh):
    placed = (P("ctx", "ch"), P("ctx", "ch"), P(None, "ch"), P("ch", None), P("ch", None), P("ch"))
    return jax.shard_map(
        body,
        mesh=mesh,
        in_specs=placed,
        out_specs=(P("ctx", "ch"), P("ch", None), P("ch", None), P("ch")),
        check_vma=False,
    )
```

profile of v0, /device:TPU:8, one launch (start us, length us, event | category | flops | bytes accessed | tf_op | source)
XLA Modules:
  0.0 63.8 jit_solution(14772038829831353178)
XLA Ops:
  0.6 57.7 %shard_map.93 = (bf16[256,256]{1,0:T(8,128)(2,1)}, f32[16,256]{1,0:T(8,128)}, f32[16,256]{1,0:T(8,128)}, f32[1,256]{1,0:T(1,128)}) custom-call(bf16[256,256]{1,0:T(8,128)(2,1)} %sig_h.1, bf16[256,512]{1,0:T(8,128)(2,1)} %up_h.1, bf16[4096,512]{1,0:T(8,128)(2,1)} %w_h.1, f32[16,256]{1,0:T(8,128)} %bitcast.6, f32[16,256]{1,0:T(8,128)} %bitcast.7, ...), custom_call_target="tpu_custom_call" | custom-call | tf_op jit(solution)/shard_map/pallas_call | solution.py:311
  58.4 1.6 %copy.14 = bf16[256,256]{1,0:T(8,128)(2,1)} copy(bf16[256,256]{1,0:T(8,128)(2,1)} %get-tuple-element.16) | data formatting | bytes 262144
  59.9 1.3 %copy.15 = f32[256,16]{0,1:T(8,128)} copy(f32[256,16]{0,1:T(8,128)} %bitcast.9) | data formatting | bytes 32768
  61.3 1.3 %copy.16 = f32[256,16]{0,1:T(8,128)} copy(f32[256,16]{0,1:T(8,128)} %bitcast.8) | data formatting | bytes 32768
  62.6 1.2 %copy.17 = f32[256]{0:T(256)} copy(f32[256]{0:T(256)} %bitcast.11) | data formatting | bytes 2048
where the time goes:
time: 64.1 us; the launch traced here: 63.8 us
  Pallas kernels  57.7 us (90%)
  local copies, waits for them, and re-layouts  5.41 us (8%)
    pallas_call x1, Pallas kernels, body(): pl.pallas_call(kernel, out_shape=(jax.ShapeDtypeStruct((tokens, width), B...  57.7 us
    unnamed x4, local copies, waits for them, and re-layouts  5.41 us

commit v1 on v0

v1 whole, which is shorter than its diff:
```python
import functools

import jax
import jax.numpy as jnp
from jax import lax
from jax.experimental import pallas as pl
from jax.experimental.pallas import tpu as pltpu
from jax.sharding import PartitionSpec as P

MESH = pl.DeviceIdType.MESH
F32 = jnp.float32
BF16 = jnp.bfloat16
RING = 8
FAR_WAY = ((4, 1), (4, 0), (3, 1), (3, 0), (2, 1), (2, 0), (1, 1), (1, 0))
NEAR_WAY = FAR_WAY[2:]
SENDS = len(FAR_WAY) + len(NEAR_WAY)


def kernel(
    sig_h, up_h, w_h, res_h, dec_h, skip_h,
    base_o, small_o,
    sig_v, up_v, w_v, res_v, dec_v, skip_v,
    sig_f, pair_s, pair_r, own, ring_s, ring_r, gc, yl,
    early_s, late_s, early_x, late_x, early_z, late_z, jumps, local_in, back, full,
    local_sem, w_sem, pair_ss, pair_rs, ring_ss, ring_rs,
    xe_ss, xe_rs, xl_ss, xl_rs, ze_ss, ze_rs, zl_ss, zl_rs, b_ss, b_rs,
):
    tokens, width = sig_h.shape
    half_rows = tokens // 2
    lanes = width // 2
    modes = res_h.shape[0]
    share = 2 * modes // RING
    per_half = RING // 2
    length = tokens * RING * RING
    ctx = lax.axis_index("ctx")
    ch = lax.axis_index("ch")
    z, x = lax.div(ctx, RING), lax.rem(ctx, RING)
    y, core = lax.div(ch, 2), lax.rem(ch, 2)

    def at_x(step):
        return (z * RING + lax.rem(x + step, RING), ch)

    def at_z(step):
        return (lax.rem(z + step, RING) * RING + x, ch)

    def at_y(step):
        return (ctx, lax.rem(y + step, RING) * 2 + core)

    partner = (ctx, y * 2 + 1 - core)
    up_ring = 1 + core * (RING - 2)

    barrier = pltpu.get_barrier_semaphore()
    peers = [partner, at_y(1), at_y(RING - 1)]
    peers += [at_x(step) for step in range(1, RING)] + [at_z(step) for step in range(1, RING)]
    for peer in peers:
        pl.semaphore_signal(barrier, inc=1, device_id=peer, device_id_type=MESH)

    def w_copy(index):
        offset = (index + 1) // 2
        dest = lax.rem(y + (4 - offset if index % 2 else 4 + offset), RING)
        return pltpu.make_async_copy(
            w_h.at[pl.ds(dest * 2 * width, 2 * width), :], w_v.at[index], w_sem.at[index]
        )

    loads = [
        pltpu.make_async_copy(src, dst, local_sem.at[n])
        for n, (src, dst) in enumerate(
            ((up_h, up_v), (dec_h, dec_v), (res_h, res_v), (skip_h, skip_v), (sig_h, sig_v))
        )
    ]
    loads[0].start()
    w_copy(0).start()
    w_copy(1).start()
    for load in loads[1:]:
        load.start()
    for index in range(2, RING):
        w_copy(index).start()
    for load in loads:
        load.wait()
    pole = jnp.exp(dec_v[...] * (-1.0 / length))
    pole_block = jnp.exp(dec_v[...] * (-float(tokens) / length))
    gain = res_v[...] * (1.0 / length**0.5)
    small_o[pl.ds(modes, modes), :] = pole
    sig_f[...] = sig_v[...].astype(F32)
    zero = jnp.zeros((modes, width), F32)

    def piece(part, peer):
        first, cols = (peer % per_half) * share, (peer // per_half) * lanes
        return part[first : first + share, cols : cols + lanes]

    for peer in range(RING):
        jumps[peer, 0:share, :] = piece(pole_block, peer)
    pl.semaphore_wait(barrier, len(peers))

    def pair_copy(index):
        return pltpu.make_async_remote_copy(
            src_ref=pair_s.at[index], dst_ref=pair_r.at[index],
            send_sem=pair_ss.at[index], recv_sem=pair_rs.at[index],
            device_id=partner, device_id_type=MESH,
        )

    def product(index):
        w_copy(index).wait()
        for mine in (0, 1):
            side = lax.rem(core + 1 + mine, 2) * width
            part = lax.dot_general(
                up_v[...], w_v[index, pl.ds(pl.multiple_of(side, width), width), :],
                (((1,), (1,)), ((), ())), preferred_element_type=F32,
            )
            if mine:
                own[index] = part
            else:
                pair_s[index] = part.astype(BF16)
                pair_copy(index).start()

    def ring_copy(far, send):
        slot = send if far else send + len(FAR_WAY)
        return pltpu.make_async_remote_copy(
            src_ref=ring_s.at[slot], dst_ref=ring_r.at[slot],
            send_sem=ring_ss.at[slot], recv_sem=ring_rs.at[slot],
            device_id=at_y(up_ring if far else RING - up_ring), device_id_type=MESH,
        )

    arrived = set()

    def chip_sum(far, dist, half):
        if dist == 0:
            index = RING - 1
        elif dist == per_half:
            index = 0
        else:
            index = 2 * (per_half - dist) + (core - 1 if far else -core)
        if (far, dist) not in arrived:
            arrived.add((far, dist))
            pair_copy(index).wait_recv()
        span = pl.ds(half * half_rows, half_rows)
        return own[index, span, :] + pair_r[index, span, :].astype(F32)

    def incoming_sum(far, send):
        ring_copy(far, send).wait_recv()
        return ring_r[send if far else send + len(FAR_WAY)].astype(F32)

    def ring_send(far, send):
        dist, half = (FAR_WAY if far else NEAR_WAY)[send]
        total = chip_sum(far, dist, half)
        if send >= 2:
            total = total + incoming_sum(far, send - 2)
        ring_s[send if far else send + len(FAR_WAY)] = total.astype(BF16)
        ring_copy(far, send).start()

    product(0)
    product(1)
    product(2)
    ring_send(True, 0)
    ring_send(True, 1)
    product(3)
    product(4)
    ring_send(False, 0)
    ring_send(False, 1)
    product(5)
    product(6)
    product(7)

    def signal_steps(group, carry):
        state, slope = carry
        for step in range(8):
            row = sig_f[pl.ds(group * 8 + step, 1), :]
            state = (state + row) * pole
            slope = slope * pole + state
        return state, slope

    sig_state, sig_slope = lax.fori_loop(0, tokens // 8, signal_steps, (zero, zero))
    for peer in range(RING):
        early_s[peer] = jnp.concatenate([piece(sig_state, peer), piece(sig_slope, peer)], axis=0)

    def x_copy(step, early):
        peer = lax.rem(x + step, RING)
        src, dst, ss, rs = (early_s, early_x, xe_ss, xe_rs) if early else (late_s, late_x, xl_ss, xl_rs)
        return pltpu.make_async_remote_copy(
            src_ref=src.at[peer], dst_ref=dst.at[x], send_sem=ss.at[step], recv_sem=rs.at[step],
            device_id=at_x(step), device_id_type=MESH,
        )

    def z_copy(step, early):
        ref, ss, rs = (early_z, ze_ss, ze_rs) if early else (late_z, zl_ss, zl_rs)
        return pltpu.make_async_remote_copy(
            src_ref=ref.at[z], dst_ref=ref.at[z], send_sem=ss.at[step], recv_sem=rs.at[step],
            device_id=at_z(step), device_id_type=MESH,
        )

    for step in range(1, RING):
        x_copy(step, True).start()
    early_x[x] = early_s[x]

    ring_send(True, 2)
    ring_send(True, 3)
    ring_send(False, 2)
    ring_send(False, 3)
    ring_send(True, 4)
    ring_send(True, 5)
    ring_send(False, 4)
    ring_send(False, 5)

    for step in range(1, RING):
        x_copy(step, True).wait_recv()
    jump = jumps[x, 0:share, :]
    empty = jnp.zeros((share, lanes), F32)
    sig_state, sig_slope = empty, empty
    for block in range(RING):
        sig_slope = early_x[block, share : 2 * share, :] + jump * (sig_slope + tokens * sig_state)
        sig_state = early_x[block, 0:share, :] + jump * sig_state
    early_z[z] = jnp.concatenate([sig_state, sig_slope], axis=0)
    for step in range(1, RING):
        z_copy(step, True).start()

    ring_send(True, 6)
    ring_send(True, 7)

    def gradient_steps(last, group, carry):
        state, slope, res_sum, dec_sum = carry
        for step in range(8):
            pos = last - (group * 8 + step)
            grad = gc[pl.ds(pos, 1), :]
            row = sig_f[pl.ds(pos, 1), :]
            moved = state * pole
            state = grad + moved
            slope = slope * pole + moved
            res_sum = res_sum + row * state
            dec_sum = dec_sum + row * slope
            yl[pl.ds(pos, 1), :] = jnp.sum(gain * state, axis=0, keepdims=True)
        return state, slope, res_sum, dec_sum

    carry = (zero, zero, zero, zero)
    skip_sum = jnp.zeros((1, width), F32)
    for half in (1, 0):
        total = chip_sum(None, 0, half)
        for far, way in ((False, NEAR_WAY), (True, FAR_WAY)):
            total = total + incoming_sum(far, len(way) - 1 - half)
        total = total.astype(BF16).astype(F32)
        span = pl.ds(half * half_rows, half_rows)
        gc[span, :] = total
        skip_sum = skip_sum + jnp.sum(total * sig_f[span, :], axis=0, keepdims=True)
        carry = lax.fori_loop(
            0, half_rows // 8, functools.partial(gradient_steps, (half + 1) * half_rows - 1), carry
        )
    state, slope, res_sum, dec_sum = carry

    skip_rows = jnp.broadcast_to(skip_sum, (8, width))
    for peer in range(RING):
        cols = (peer // per_half) * lanes
        late_s[peer, 0:8, :] = jnp.concatenate([piece(state, peer), piece(slope, peer)], axis=0).astype(BF16)
        late_s[peer, 8:16, :] = jnp.concatenate([piece(res_sum, peer), piece(dec_sum, peer)], axis=0).astype(BF16)
        late_s[peer, 16:24, :] = skip_rows[:, cols : cols + lanes].astype(BF16)
    for step in range(1, RING):
        x_copy(step, False).start()
    late_x[x] = late_s[x]
    yl[...] = yl[...] + skip_v[...] * gc[...]
    base_copy = pltpu.make_async_copy(yl, base_o, local_sem.at[len(loads)])
    base_copy.start()
    for step in range(1, RING):
        x_copy(step, False).wait_recv()

    def parts_of(early, late, index):
        sums = late[index].astype(F32)
        early_part = early[index]
        return (
            sums[0:share], sums[share : 2 * share], sums[2 * share : 3 * share], sums[3 * share : 4 * share],
            sums[4 * share : 5 * share], early_part[0:share], early_part[share : 2 * share],
        )

    def join(parts, carry, jump, span):
        own_state, own_slope, own_res, own_dec, own_skip, sig_state, sig_slope = parts
        state, slope, res_sum, dec_sum, skip_sum = carry
        return (
            own_state + jump * state,
            own_slope + jump * (slope + span * state),
            res_sum + own_res + state * sig_state,
            dec_sum + own_dec + slope * sig_state + state * sig_slope,
            skip_sum + own_skip,
        )

    carry = (empty,) * 5
    for block in reversed(range(RING)):
        local_in[block] = carry[0]
        carry = join(parts_of(early_x, late_x, block), carry, jump, float(tokens))
    late_z[z, 0:8, :] = jnp.concatenate(carry[0:2], axis=0).astype(BF16)
    late_z[z, 8:16, :] = jnp.concatenate(carry[2:4], axis=0).astype(BF16)
    late_z[z, 16:24, :] = jnp.concatenate([carry[4], carry[4]], axis=0).astype(BF16)
    for step in range(1, RING):
        z_copy(step, False).start()
    row_jump = jump * jump
    row_jump = row_jump * row_jump
    row_jump = row_jump * row_jump
    for step in range(1, RING):
        z_copy(step, True).wait_recv()
    for step in range(1, RING):
        z_copy(step, False).wait_recv()

    incoming = empty
    carry = (empty,) * 5
    for row in reversed(range(RING)):
        incoming = jnp.where(z == row, carry[0], incoming)
        carry = join(parts_of(early_z, late_z, row), carry, row_jump, float(tokens * RING))
    for block in reversed(range(RING)):
        back[block, 0:8, :] = jnp.concatenate([local_in[block] + incoming, carry[2]], axis=0)
        back[block, 8:16, :] = jnp.concatenate([carry[3], carry[4]], axis=0)
        incoming = incoming * jump

    def b_copy(step):
        return pltpu.make_async_remote_copy(
            src_ref=back.at[lax.rem(x + step, RING)], dst_ref=full.at[x],
            send_sem=b_ss.at[step], recv_sem=b_rs.at[step],
            device_id=at_x(step), device_id_type=MESH,
        )

    for step in range(1, RING):
        b_copy(step).start()
    full[x] = back[x]
    base_copy.wait()
    for index in range(RING):
        pair_copy(index).wait_send()
    for far, way in ((True, FAR_WAY), (False, NEAR_WAY)):
        for send in range(len(way)):
            ring_copy(far, send).wait_send()
    for step in range(1, RING):
        for early in (True, False):
            x_copy(step, early).wait_send()
            z_copy(step, early).wait_send()
    for step in range(1, RING):
        b_copy(step).wait_recv()

    for peer in range(RING):
        cols = pl.ds((peer // per_half) * lanes, lanes)
        first = (peer % per_half) * share
        for line in range(3):
            small_o[pl.ds((0, 2, 3)[line] * modes + first, share), cols] = full[
                peer, line * share : (line + 1) * share, :
            ]
        if peer % per_half == 0:
            small_o[pl.ds(4 * modes, 8), cols] = full[peer, 8:16, :]
    here = pl.ds(0, modes)
    small_o[here, :] = small_o[here, :] * gain
    here = pl.ds(2 * modes, modes)
    small_o[here, :] = small_o[here, :] * (1.0 / length)
    here = pl.ds(3 * modes, modes)
    small_o[here, :] = small_o[here, :] * (-1.0 / length) * (1.0 / length) * res_v[...]
    here = pl.ds(4 * modes, 8)
    small_o[here, :] = small_o[here, :] * (1.0 / length**0.5)
    for step in range(1, RING):
        b_copy(step).wait_send()


def finish(base, small, out, res_o, dec_o, skip_o, late):
    tokens = base.shape[0]
    modes = res_o.shape[0]
    res_o[...] = small[pl.ds(2 * modes, modes), :]
    dec_o[...] = small[pl.ds(3 * modes, modes), :]
    skip_o[...] = small[pl.ds(4 * modes + 4, 1), :]
    pole = small[pl.ds(modes, modes), :]

    def late_steps(group, term):
        for step in range(8):
            term = term * pole
            late[pl.ds(tokens - 1 - (group * 8 + step), 1), :] = jnp.sum(term, axis=0, keepdims=True)
        return term

    lax.fori_loop(0, tokens // 8, late_steps, small[pl.ds(0, modes), :])
    out[...] = (base[...] + late[...]).astype(BF16)


def body(signal, upstream, out_weight, residues, decays, skip_gain):
    tokens, width = signal.shape
    features = upstream.shape[1]
    modes = residues.shape[1]
    lanes = width // 2
    share = 2 * modes // RING
    any_ref = pl.BlockSpec(memory_space=pl.ANY)
    in_vmem = pl.BlockSpec(memory_space=pltpu.VMEM)
    dma = pltpu.SemaphoreType.DMA
    base, small = pl.pallas_call(
        kernel,
        out_shape=(
            jax.ShapeDtypeStruct((tokens, width), F32),
            jax.ShapeDtypeStruct((4 * modes + 8, width), F32),
        ),
        in_specs=[any_ref] * 6,
        out_specs=(any_ref, in_vmem),
        scratch_shapes=[
            pltpu.VMEM((tokens, width), BF16),
            pltpu.VMEM((tokens, features), BF16),
            pltpu.VMEM((RING, 2 * width, features), BF16),
            pltpu.VMEM((modes, width), F32),
            pltpu.VMEM((modes, width), F32),
            pltpu.VMEM((1, width), F32),
            pltpu.VMEM((tokens, width), F32),
            pltpu.VMEM((RING, tokens, width), BF16),
            pltpu.VMEM((RING, tokens, width), BF16),
            pltpu.VMEM((RING, tokens, width), F32),
            pltpu.VMEM((SENDS, tokens // 2, width), BF16),
            pltpu.VMEM((SENDS, tokens // 2, width), BF16),
            pltpu.VMEM((tokens, width), F32),
            pltpu.VMEM((tokens, width), F32),
            pltpu.VMEM((RING, 2 * share, lanes), F32),
            pltpu.VMEM((RING, 6 * share, lanes), BF16),
            pltpu.VMEM((RING, 2 * share, lanes), F32),
            pltpu.VMEM((RING, 6 * share, lanes), BF16),
            pltpu.VMEM((RING, 2 * share, lanes), F32),
            pltpu.VMEM((RING, 6 * share, lanes), BF16),
            pltpu.VMEM((RING, 2 * share, lanes), F32),
            pltpu.VMEM((RING, share, lanes), F32),
            pltpu.VMEM((RING, 4 * share, lanes), F32),
            pltpu.VMEM((RING, 4 * share, lanes), F32),
            dma((6,)), dma((RING,)), dma((RING,)), dma((RING,)), dma((SENDS,)), dma((SENDS,)),
        ] + [dma((RING,))] * 10,
        compiler_params=pltpu.CompilerParams(collective_id=0, has_side_effects=True),
    )(signal, upstream, out_weight, residues.T, decays.T, skip_gain.reshape(1, width))
    grad_signal, res_t, dec_t, skip = pl.pallas_call(
        finish,
        out_shape=(
            jax.ShapeDtypeStruct((tokens, width), BF16),
            jax.ShapeDtypeStruct((modes, width), F32),
            jax.ShapeDtypeStruct((modes, width), F32),
            jax.ShapeDtypeStruct((1, width), F32),
        ),
        in_specs=[in_vmem] * 2,
        out_specs=(in_vmem,) * 4,
        scratch_shapes=[pltpu.VMEM((tokens, width), F32)],
    )(base, small)
    return grad_signal, res_t.T, dec_t.T, skip.reshape(width)


def solution(mesh):
    placed = (P("ctx", "ch"), P("ctx", "ch"), P(None, "ch"), P("ch", None), P("ch", None), P("ch"))
    return jax.shard_map(
        body,
        mesh=mesh,
        in_specs=placed,
        out_specs=(P("ctx", "ch"), P("ch", None), P("ch", None), P("ch")),
        check_vma=False,
    )
```

time: 64.1 us -> 60.4 us (0.942)
  the two profiles are of different devices: /device:TPU:8 before, /device:TPU:16 now
where the time goes in v1:
time: 60.4 us; the launch traced here: 60.3 us
  Pallas kernels  59.6 us (99%)
  between operations  0.64 us (1%)
    pallas_call x1, Pallas kernels, body(): pl.pallas_call(kernel, out_shape=(jax.ShapeDtypeStruct((tokens, width), F...  57.1 us
    pallas_call x1, Pallas kernels, body(): pl.pallas_call(finish, out_shape=(jax.ShapeDtypeStruct((tokens, width), B...  2.56 us

profile of v1, /device:TPU:16, one launch (start us, length us, event | category | flops | bytes accessed | tf_op | source)
XLA Modules:
  0.0 60.3 jit_solution(5102221341799051776)
XLA Ops:
  0.6 57.1 %shard_map.93 = (f32[256,256]{1,0:T(8,128)}, f32[72,256]{1,0:T(8,128)}) custom-call(bf16[256,256]{1,0:T(8,128)(2,1)} %sig_h.1, bf16[256,512]{1,0:T(8,128)(2,1)} %up_h.1, bf16[4096,512]{1,0:T(8,128)(2,1)} %w_h.1, f32[16,256]{1,0:T(8,128)} %bitcast.6, f32[16,256]{1,0:T(8,128)} %bitcast.7, f32[1,256]{1,0:T(1,128)} %bitcast.8), custom_call_target="tpu_custom_call" | custom-call | tf_op jit(solution)/shard_map/pallas_call | solution.py:380
  57.7 2.6 %shard_map.94 = (bf16[256,256]{1,0:T(8,128)(2,1)}, f32[16,256]{1,0:T(8,128)}, f32[16,256]{1,0:T(8,128)}, f32[1,256]{1,0:T(1,128)}) custom-call(f32[256,256]{1,0:T(8,128)} %get-tuple-element.10.base, f32[72,256]{1,0:T(8,128)} %get-tuple-element.11.small), custom_call_target="tpu_custom_call" | custom-call | tf_op jit(solution)/shard_map/pallas_call | solution.py:417

commit v2 on v1

--- a/solution.py
+++ b/solution.py
@@ -11,8 +11,10 @@
 F32 = jnp.float32
 BF16 = jnp.bfloat16
 RING = 8
-FAR_WAY = ((4, 1), (4, 0), (3, 1), (3, 0), (2, 1), (2, 0), (1, 1), (1, 0))
-NEAR_WAY = FAR_WAY[2:]
+PARTS = 4
+PEER_ORDER = (4, 3, 5, 2, 6, 1, 7)
+FAR_WAY = tuple((dist, part) for dist in (4, 3, 2, 1) for part in reversed(range(PARTS)))
+NEAR_WAY = FAR_WAY[PARTS:]
 SENDS = len(FAR_WAY) + len(NEAR_WAY)
 
 
@@ -26,7 +28,7 @@
     xe_ss, xe_rs, xl_ss, xl_rs, ze_ss, ze_rs, zl_ss, zl_rs, b_ss, b_rs,
 ):
     tokens, width = sig_h.shape
-    half_rows = tokens // 2
+    part_rows = tokens // PARTS
     lanes = width // 2
     modes = res_h.shape[0]
     share = 2 * modes // RING
@@ -90,7 +92,6 @@
 
     for peer in range(RING):
         jumps[peer, 0:share, :] = piece(pole_block, peer)
-    pl.semaphore_wait(barrier, len(peers))
 
     def pair_copy(index):
         return pltpu.make_async_remote_copy(
@@ -111,7 +112,8 @@
                 own[index] = part
             else:
                 pair_s[index] = part.astype(BF16)
-                pair_copy(index).start()
+                if index > 0:
+                    pair_copy(index).start()
 
     def ring_copy(far, send):
         slot = send if far else send + len(FAR_WAY)
@@ -123,7 +125,7 @@
 
     arrived = set()
 
-    def chip_sum(far, dist, half):
+    def chip_sum(far, dist, part):
         if dist == 0:
             index = RING - 1
         elif dist == per_half:
@@ -133,7 +135,7 @@
         if (far, dist) not in arrived:
             arrived.add((far, dist))
             pair_copy(index).wait_recv()
-        span = pl.ds(half * half_rows, half_rows)
+        span = pl.ds(part * part_rows, part_rows)
         return own[index, span, :] + pair_r[index, span, :].astype(F32)
 
     def incoming_sum(far, send):
@@ -141,25 +143,12 @@
         return ring_r[send if far else send + len(FAR_WAY)].astype(F32)
 
     def ring_send(far, send):
-        dist, half = (FAR_WAY if far else NEAR_WAY)[send]
-        total = chip_sum(far, dist, half)
-        if send >= 2:
-            total = total + incoming_sum(far, send - 2)
+        dist, part = (FAR_WAY if far else NEAR_WAY)[send]
+        total = chip_sum(far, dist, part)
+        if send >= PARTS:
+            total = total + incoming_sum(far, send - PARTS)
         ring_s[send if far else send + len(FAR_WAY)] = total.astype(BF16)
         ring_copy(far, send).start()
-
-    product(0)
-    product(1)
-    product(2)
-    ring_send(True, 0)
-    ring_send(True, 1)
-    product(3)
-    product(4)
-    ring_send(False, 0)
-    ring_send(False, 1)
-    product(5)
-    product(6)
-    product(7)
 
     def signal_steps(group, carry):
         state, slope = carry
@@ -169,9 +158,9 @@
             slope = slope * pole + state
         return state, slope
 
-    sig_state, sig_slope = lax.fori_loop(0, tokens // 8, signal_steps, (zero, zero))
-    for peer in range(RING):
-        early_s[peer] = jnp.concatenate([piece(sig_state, peer), piece(sig_slope, peer)], axis=0)
+    def signal_part(part, carry):
+        groups = tokens // 8 // 4
+        return lax.fori_loop(part * groups, (part + 1) * groups, signal_steps, carry)
 
     def x_copy(step, early):
         peer = lax.rem(x + step, RING)
@@ -188,33 +177,37 @@
             device_id=at_z(step), device_id_type=MESH,
         )
 
-    for step in range(1, RING):
-        x_copy(step, True).start()
+    product(0)
+    pl.semaphore_wait(barrier, len(peers))
+    pair_copy(0).start()
+    product(1)
+    product(2)
+    for send in range(PARTS):
+        ring_send(True, send)
+    product(3)
+    product(4)
+    for send in range(PARTS):
+        ring_send(False, send)
+    product(5)
+    product(6)
+    product(7)
+    signal = signal_part(0, (zero, zero))
+    for send in range(PARTS, 3 * PARTS):
+        ring_send(True, send)
+        ring_send(False, send)
+        if send == PARTS + 1:
+            signal = signal_part(1, signal)
+        if send == 2 * PARTS - 1:
+            signal = signal_part(2, signal)
+        if send == 2 * PARTS + 1:
+            signal = signal_part(3, signal)
+            for peer in range(RING):
+                early_s[peer] = jnp.concatenate([piece(signal[0], peer), piece(signal[1], peer)], axis=0)
+            for step in PEER_ORDER:
+                x_copy(step, True).start()
     early_x[x] = early_s[x]
-
-    ring_send(True, 2)
-    ring_send(True, 3)
-    ring_send(False, 2)
-    ring_send(False, 3)
-    ring_send(True, 4)
-    ring_send(True, 5)
-    ring_send(False, 4)
-    ring_send(False, 5)
-
-    for step in range(1, RING):
-        x_copy(step, True).wait_recv()
-    jump = jumps[x, 0:share, :]
-    empty = jnp.zeros((share, lanes), F32)
-    sig_state, sig_slope = empty, empty
-    for block in range(RING):
-        sig_slope = early_x[block, share : 2 * share, :] + jump * (sig_slope + tokens * sig_state)
-        sig_state = early_x[block, 0:share, :] + jump * sig_state
-    early_z[z] = jnp.concatenate([sig_state, sig_slope], axis=0)
-    for step in range(1, RING):
-        z_copy(step, True).start()
-
-    ring_send(True, 6)
-    ring_send(True, 7)
+    for send in range(3 * PARTS, 4 * PARTS):
+        ring_send(True, send)
 
     def gradient_steps(last, group, carry):
         state, slope, res_sum, dec_sum = carry
@@ -232,16 +225,16 @@
 
     carry = (zero, zero, zero, zero)
     skip_sum = jnp.zeros((1, width), F32)
-    for half in (1, 0):
-        total = chip_sum(None, 0, half)
+    for part in reversed(range(PARTS)):
+        total = chip_sum(None, 0, part)
         for far, way in ((False, NEAR_WAY), (True, FAR_WAY)):
-            total = total + incoming_sum(far, len(way) - 1 - half)
+            total = total + incoming_sum(far, len(way) - 1 - part)
         total = total.astype(BF16).astype(F32)
-        span = pl.ds(half * half_rows, half_rows)
+        span = pl.ds(part * part_rows, part_rows)
         gc[span, :] = total
         skip_sum = skip_sum + jnp.sum(total * sig_f[span, :], axis=0, keepdims=True)
         carry = lax.fori_loop(
-            0, half_rows // 8, functools.partial(gradient_steps, (half + 1) * half_rows - 1), carry
+            0, part_rows // 8, functools.partial(gradient_steps, (part + 1) * part_rows - 1), carry
         )
     state, slope, res_sum, dec_sum = carry
 
@@ -251,9 +244,21 @@
         late_s[peer, 0:8, :] = jnp.concatenate([piece(state, peer), piece(slope, peer)], axis=0).astype(BF16)
         late_s[peer, 8:16, :] = jnp.concatenate([piece(res_sum, peer), piece(dec_sum, peer)], axis=0).astype(BF16)
         late_s[peer, 16:24, :] = skip_rows[:, cols : cols + lanes].astype(BF16)
-    for step in range(1, RING):
+    for step in PEER_ORDER:
         x_copy(step, False).start()
     late_x[x] = late_s[x]
+
+    for step in range(1, RING):
+        x_copy(step, True).wait_recv()
+    jump = jumps[x, 0:share, :]
+    empty = jnp.zeros((share, lanes), F32)
+    sig_state, sig_slope = empty, empty
+    for block in range(RING):
+        sig_slope = early_x[block, share : 2 * share, :] + jump * (sig_slope + tokens * sig_state)
+        sig_state = early_x[block, 0:share, :] + jump * sig_state
+    early_z[z] = jnp.concatenate([sig_state, sig_slope], axis=0)
+    for step in PEER_ORDER:
+        z_copy(step, True).start()
     yl[...] = yl[...] + skip_v[...] * gc[...]
     base_copy = pltpu.make_async_copy(yl, base_o, local_sem.at[len(loads)])
     base_copy.start()
@@ -286,7 +291,7 @@
     late_z[z, 0:8, :] = jnp.concatenate(carry[0:2], axis=0).astype(BF16)
     late_z[z, 8:16, :] = jnp.concatenate(carry[2:4], axis=0).astype(BF16)
     late_z[z, 16:24, :] = jnp.concatenate([carry[4], carry[4]], axis=0).astype(BF16)
-    for step in range(1, RING):
+    for step in PEER_ORDER:
         z_copy(step, False).start()
     row_jump = jump * jump
     row_jump = row_jump * row_jump
@@ -302,8 +307,8 @@
         incoming = jnp.where(z == row, carry[0], incoming)
         carry = join(parts_of(early_z, late_z, row), carry, row_jump, float(tokens * RING))
     for block in reversed(range(RING)):
-        back[block, 0:8, :] = jnp.concatenate([local_in[block] + incoming, carry[2]], axis=0)
-        back[block, 8:16, :] = jnp.concatenate([carry[3], carry[4]], axis=0)
+        back[block, 0:8, :] = jnp.concatenate([local_in[block] + incoming, carry[2]], axis=0).astype(BF16)
+        back[block, 8:16, :] = jnp.concatenate([carry[3], carry[4]], axis=0).astype(BF16)
         incoming = incoming * jump
 
     def b_copy(step):
@@ -313,7 +318,7 @@
             device_id=at_x(step), device_id_type=MESH,
         )
 
-    for step in range(1, RING):
+    for step in PEER_ORDER:
         b_copy(step).start()
     full[x] = back[x]
     base_copy.wait()
@@ -332,12 +337,11 @@
     for peer in range(RING):
         cols = pl.ds((peer // per_half) * lanes, lanes)
         first = (peer % per_half) * share
+        sums = full[peer].astype(F32)
         for line in range(3):
-            small_o[pl.ds((0, 2, 3)[line] * modes + first, share), cols] = full[
-                peer, line * share : (line + 1) * share, :
-            ]
+            small_o[pl.ds((0, 2, 3)[line] * modes + first, share), cols] = sums[line * share : (line + 1) * share]
         if peer % per_half == 0:
-            small_o[pl.ds(4 * modes, 8), cols] = full[peer, 8:16, :]
+            small_o[pl.ds(4 * modes, 8), cols] = sums[2 * share : 4 * share]
     here = pl.ds(0, modes)
     small_o[here, :] = small_o[here, :] * gain
     here = pl.ds(2 * modes, modes)
@@ -396,8 +400,8 @@
             pltpu.VMEM((RING, tokens, width), BF16),
             pltpu.VMEM((RING, tokens, width), BF16),
             pltpu.VMEM((RING, tokens, width), F32),
-            pltpu.VMEM((SENDS, tokens // 2, width), BF16),
-            pltpu.VMEM((SENDS, tokens // 2, width), BF16),
+            pltpu.VMEM((SENDS, tokens // PARTS, width), BF16),
+            pltpu.VMEM((SENDS, tokens // PARTS, width), BF16),
             pltpu.VMEM((tokens, width), F32),
             pltpu.VMEM((tokens, width), F32),
             pltpu.VMEM((RING, 2 * share, lanes), F32),
@@ -408,8 +412,8 @@
             pltpu.VMEM((RING, 6 * share, lanes), BF16),
             pltpu.VMEM((RING, 2 * share, lanes), F32),
             pltpu.VMEM((RING, share, lanes), F32),
-            pltpu.VMEM((RING, 4 * share, lanes), F32),
-            pltpu.VMEM((RING, 4 * share, lanes), F32),
+            pltpu.VMEM((RING, 4 * share, lanes), BF16),
+            pltpu.VMEM((RING, 4 * share, lanes), BF16),
             dma((6,)), dma((RING,)), dma((RING,)), dma((RING,)), dma((SENDS,)), dma((SENDS,)),
         ] + [dma((RING,))] * 10,
         compiler_params=pltpu.CompilerParams(collective_id=0, has_side_effects=True),

time: 60.4 us -> 57.7 us (0.955)
  the two profiles are of different devices: /device:TPU:16 before, /device:TPU:2 now
where the time goes in v2:
time: 57.7 us; the launch traced here: 57.6 us
  Pallas kernels  56.9 us (99%)
  between operations  0.64 us (1%)
    pallas_call x1, Pallas kernels, body(): pl.pallas_call(kernel, out_shape=(jax.ShapeDtypeStruct((tokens, width), F...  54.4 us
    pallas_call x1, Pallas kernels, body(): pl.pallas_call(finish, out_shape=(jax.ShapeDtypeStruct((tokens, width), B...  2.56 us

profile of v2, /device:TPU:2, one launch (start us, length us, event | category | flops | bytes accessed | tf_op | source)
XLA Modules:
  0.0 57.6 jit_solution(17479204834095222252)
XLA Ops:
  0.6 54.4 %shard_map.93 = (f32[256,256]{1,0:T(8,128)}, f32[72,256]{1,0:T(8,128)}) custom-call(bf16[256,256]{1,0:T(8,128)(2,1)} %sig_h.1, bf16[256,512]{1,0:T(8,128)(2,1)} %up_h.1, bf16[4096,512]{1,0:T(8,128)(2,1)} %w_h.1, f32[16,256]{1,0:T(8,128)} %bitcast.6, f32[16,256]{1,0:T(8,128)} %bitcast.7, f32[1,256]{1,0:T(1,128)} %bitcast.8), custom_call_target="tpu_custom_call" | custom-call | tf_op jit(solution)/shard_map/pallas_call | solution.py:384
  55.0 2.6 %shard_map.94 = (bf16[256,256]{1,0:T(8,128)(2,1)}, f32[16,256]{1,0:T(8,128)}, f32[16,256]{1,0:T(8,128)}, f32[1,256]{1,0:T(1,128)}) custom-call(f32[256,256]{1,0:T(8,128)} %get-tuple-element.10.base, f32[72,256]{1,0:T(8,128)} %get-tuple-element.11.small), custom_call_target="tpu_custom_call" | custom-call | tf_op jit(solution)/shard_map/pallas_call | solution.py:421

commit v3 on v2

--- a/solution.py
+++ b/solution.py
@@ -77,21 +77,10 @@
         load.start()
     for index in range(2, RING):
         w_copy(index).start()
-    for load in loads:
-        load.wait()
-    pole = jnp.exp(dec_v[...] * (-1.0 / length))
-    pole_block = jnp.exp(dec_v[...] * (-float(tokens) / length))
-    gain = res_v[...] * (1.0 / length**0.5)
-    small_o[pl.ds(modes, modes), :] = pole
-    sig_f[...] = sig_v[...].astype(F32)
-    zero = jnp.zeros((modes, width), F32)
 
     def piece(part, peer):
         first, cols = (peer % per_half) * share, (peer // per_half) * lanes
         return part[first : first + share, cols : cols + lanes]
-
-    for peer in range(RING):
-        jumps[peer, 0:share, :] = piece(pole_block, peer)
 
     def pair_copy(index):
         return pltpu.make_async_remote_copy(
@@ -150,18 +139,6 @@
         ring_s[send if far else send + len(FAR_WAY)] = total.astype(BF16)
         ring_copy(far, send).start()
 
-    def signal_steps(group, carry):
-        state, slope = carry
-        for step in range(8):
-            row = sig_f[pl.ds(group * 8 + step, 1), :]
-            state = (state + row) * pole
-            slope = slope * pole + state
-        return state, slope
-
-    def signal_part(part, carry):
-        groups = tokens // 8 // 4
-        return lax.fori_loop(part * groups, (part + 1) * groups, signal_steps, carry)
-
     def x_copy(step, early):
         peer = lax.rem(x + step, RING)
         src, dst, ss, rs = (early_s, early_x, xe_ss, xe_rs) if early else (late_s, late_x, xl_ss, xl_rs)
@@ -177,6 +154,7 @@
             device_id=at_z(step), device_id_type=MESH,
         )
 
+    loads[0].wait()
     product(0)
     pl.semaphore_wait(barrier, len(peers))
     pair_copy(0).start()
@@ -191,6 +169,30 @@
     product(5)
     product(6)
     product(7)
+
+    for load in loads[1:]:
+        load.wait()
+    pole = jnp.exp(dec_v[...] * (-1.0 / length))
+    pole_block = jnp.exp(dec_v[...] * (-float(tokens) / length))
+    gain = res_v[...] * (1.0 / length**0.5)
+    small_o[pl.ds(modes, modes), :] = pole
+    sig_f[...] = sig_v[...].astype(F32)
+    zero = jnp.zeros((modes, width), F32)
+    for peer in range(RING):
+        jumps[peer, 0:share, :] = piece(pole_block, peer)
+
+    def signal_steps(group, carry):
+        state, slope = carry
+        for step in range(8):
+            row = sig_f[pl.ds(group * 8 + step, 1), :]
+            state = (state + row) * pole
+            slope = slope * pole + state
+        return state, slope
+
+    def signal_part(part, carry):
+        groups = tokens // 8 // 4
+        return lax.fori_loop(part * groups, (part + 1) * groups, signal_steps, carry)
+
     signal = signal_part(0, (zero, zero))
     for send in range(PARTS, 3 * PARTS):
         ring_send(True, send)
@@ -378,16 +380,18 @@
     modes = residues.shape[1]
     lanes = width // 2
     share = 2 * modes // RING
+    in_hbm = pl.BlockSpec(memory_space=pltpu.HBM)
     any_ref = pl.BlockSpec(memory_space=pl.ANY)
     in_vmem = pl.BlockSpec(memory_space=pltpu.VMEM)
     dma = pltpu.SemaphoreType.DMA
+    args = (signal, upstream, out_weight, residues.T, decays.T, skip_gain.reshape(1, width))
     base, small = pl.pallas_call(
         kernel,
         out_shape=(
             jax.ShapeDtypeStruct((tokens, width), F32),
             jax.ShapeDtypeStruct((4 * modes + 8, width), F32),
         ),
-        in_specs=[any_ref] * 6,
+        in_specs=[in_hbm] * 6,
         out_specs=(any_ref, in_vmem),
         scratch_shapes=[
             pltpu.VMEM((tokens, width), BF16),
@@ -416,8 +420,10 @@
             pltpu.VMEM((RING, 4 * share, lanes), BF16),
             dma((6,)), dma((RING,)), dma((RING,)), dma((RING,)), dma((SENDS,)), dma((SENDS,)),
         ] + [dma((RING,))] * 10,
-        compiler_params=pltpu.CompilerParams(collective_id=0, has_side_effects=True),
-    )(signal, upstream, out_weight, residues.T, decays.T, skip_gain.reshape(1, width))
+        compiler_params=pltpu.CompilerParams(
+            collective_id=0, has_side_effects=True, vmem_limit_bytes=24 << 20
+        ),
+    )(*(pltpu.with_memory_space_constraint(a, pltpu.HBM) for a in args))
     grad_signal, res_t, dec_t, skip = pl.pallas_call(
         finish,
         out_shape=(
@@ -429,6 +435,7 @@
         in_specs=[in_vmem] * 2,
         out_specs=(in_vmem,) * 4,
         scratch_shapes=[pltpu.VMEM((tokens, width), F32)],
+        compiler_params=pltpu.CompilerParams(vmem_limit_bytes=8 << 20),
     )(base, small)
     return grad_signal, res_t.T, dec_t.T, skip.reshape(width)
 

time: 57.7 us -> 56 us (0.971)
  Pallas kernels: 56.9 us -> 55.2 us
    pallas_call x1, Pallas kernels: 2.56 us -> 1.6 us  [body(): pl.pallas_call(finish, out_shape=(jax.ShapeDtypeStruct((tokens, width), B...]
    pallas_call x1, Pallas kernels: 54.4 us -> 53.6 us  [body(): pl.pallas_call(kernel, out_shape=(jax.ShapeDtypeStruct((tokens, width), F...]
where the time goes in v3:
time: 56 us; the launch traced here: 55.8 us
  Pallas kernels  55.2 us (99%)
  between operations  0.64 us (1%)
    pallas_call x1, Pallas kernels, body(): pl.pallas_call(kernel, out_shape=(jax.ShapeDtypeStruct((tokens, width), F...  53.6 us
    pallas_call x1, Pallas kernels, body(): pl.pallas_call(finish, out_shape=(jax.ShapeDtypeStruct((tokens, width), B...  1.6 us

profile of v3, /device:TPU:2, one launch (start us, length us, event | category | flops | bytes accessed | tf_op | source)
XLA Modules:
  0.0 55.8 jit_solution(2628822127165258906)
XLA Ops:
  0.6 53.6 %shard_map.93 = (f32[256,256]{1,0:T(8,128)S(1)}, f32[72,256]{1,0:T(8,128)S(1)}) custom-call(bf16[256,256]{1,0:T(8,128)(2,1)} %sig_h.1, bf16[256,512]{1,0:T(8,128)(2,1)} %up_h.1, bf16[4096,512]{1,0:T(8,128)(2,1)} %w_h.1, f32[16,256]{1,0:T(8,128)} %bitcast.6, f32[16,256]{1,0:T(8,128)} %bitcast.7, f32[1,256]{1,0:T(1,128)} %bitcast.8), custom_call_target="tpu_custom_call" | custom-call | tf_op jit(solution)/shard_map/pallas_call | solution.py:388
  54.2 1.6 %shard_map.94 = (bf16[256,256]{1,0:T(8,128)(2,1)}, f32[16,256]{1,0:T(8,128)}, f32[16,256]{1,0:T(8,128)}, f32[1,256]{1,0:T(1,128)}) custom-call(f32[256,256]{1,0:T(8,128)S(1)} %get-tuple-element.10.base, f32[72,256]{1,0:T(8,128)S(1)} %get-tuple-element.11.small), custom_call_target="tpu_custom_call" | custom-call | tf_op jit(solution)/shard_map/pallas_call | solution.py:427

commit v4 on v3

--- a/solution.py
+++ b/solution.py
@@ -222,7 +222,6 @@
             slope = slope * pole + moved
             res_sum = res_sum + row * state
             dec_sum = dec_sum + row * slope
-            yl[pl.ds(pos, 1), :] = jnp.sum(gain * state, axis=0, keepdims=True)
         return state, slope, res_sum, dec_sum
 
     carry = (zero, zero, zero, zero)
@@ -261,6 +260,15 @@
     early_z[z] = jnp.concatenate([sig_state, sig_slope], axis=0)
     for step in PEER_ORDER:
         z_copy(step, True).start()
+
+    def local_steps(group, state):
+        for step in range(8):
+            pos = tokens - 1 - (group * 8 + step)
+            state = gc[pl.ds(pos, 1), :] + state * pole
+            yl[pl.ds(pos, 1), :] = jnp.sum(gain * state, axis=0, keepdims=True)
+        return state
+
+    lax.fori_loop(0, tokens // 8, local_steps, zero)
     yl[...] = yl[...] + skip_v[...] * gc[...]
     base_copy = pltpu.make_async_copy(yl, base_o, local_sem.at[len(loads)])
     base_copy.start()

time: 56 us -> 55.8 us (level)
  no operation moved by 1% of the time
where the time goes in v4:
time: 55.8 us; the launch traced here: 55.6 us
  Pallas kernels  55 us (99%)
  between operations  0.64 us (1%)
    pallas_call x1, Pallas kernels, body(): pl.pallas_call(kernel, out_shape=(jax.ShapeDtypeStruct((tokens, width), F...  53.4 us
    pallas_call x1, Pallas kernels, body(): pl.pallas_call(finish, out_shape=(jax.ShapeDtypeStruct((tokens, width), B...  1.6 us

profile of v4, /device:TPU:2, one launch (start us, length us, event | category | flops | bytes accessed | tf_op | source)
XLA Modules:
  0.0 55.6 jit_solution(193035895881109942)
XLA Ops:
  0.6 53.4 %shard_map.93 = (f32[256,256]{1,0:T(8,128)S(1)}, f32[72,256]{1,0:T(8,128)S(1)}) custom-call(bf16[256,256]{1,0:T(8,128)(2,1)} %sig_h.1, bf16[256,512]{1,0:T(8,128)(2,1)} %up_h.1, bf16[4096,512]{1,0:T(8,128)(2,1)} %w_h.1, f32[16,256]{1,0:T(8,128)} %bitcast.6, f32[16,256]{1,0:T(8,128)} %bitcast.7, f32[1,256]{1,0:T(1,128)} %bitcast.8), custom_call_target="tpu_custom_call" | custom-call | tf_op jit(solution)/shard_map/pallas_call | solution.py:396
  54.0 1.6 %shard_map.94 = (bf16[256,256]{1,0:T(8,128)(2,1)}, f32[16,256]{1,0:T(8,128)}, f32[16,256]{1,0:T(8,128)}, f32[1,256]{1,0:T(1,128)}) custom-call(f32[256,256]{1,0:T(8,128)S(1)} %get-tuple-element.10.base, f32[72,256]{1,0:T(8,128)S(1)} %get-tuple-element.11.small), custom_call_target="tpu_custom_call" | custom-call | tf_op jit(solution)/shard_map/pallas_call | solution.py:435
